TPU v7x, 128 devices: a whole 4x4x4 slice. The times are simulated.
128 devices in a mesh: tx: 4 (over z), ty: 32 (over x, y, core).
Axes of the slice: x: 4, y: 4, z: 4, core: 2. Of those that a mesh axis runs over, the one named last changes fastest.
Arguments:
- points: bfloat16 [128, 1024, 256], P(('tx', 'ty')), may hold values from -6 to 6
- counts: int32 [128], P(('tx', 'ty')), may hold values from 512 to 1024, as said below
- owner: int32 [128, 1024], P(('tx', 'ty')), may hold values from 0 to 127, as said below
- zorder: int32 [128, 2048], P(('tx', 'ty')), may hold values from 0 to 2047, as said below
- border: int32 [128, 4, 64], P(('tx', 'ty')), may hold values from 0 to 1023, as said below
- near: int32 [128, 16, 1024], P(('tx', 'ty')), may hold values from 0 to 1279, as said below
- w_near: bfloat16 [256, 256], replicated, may hold values from -0.375 to 0.375
- gain_one: float32 [256], replicated, may hold values from 0.1 to 1.9
- conv_w: bfloat16 [3, 8, 32, 32], replicated, may hold values from -0.625 to 0.625
- gain_two: float32 [256], replicated, may hold values from 0.1 to 1.9
- w_up: bfloat16 [256, 1024], replicated, may hold values from -0.375 to 0.375
- w_down: bfloat16 [1024, 256], replicated, may hold values from -0.1875 to 0.1875
- grad_out: bfloat16 [128, 1024, 256], P(('tx', 'ty')), may hold values from -6 to 6
Outputs:
- out_rows: bfloat16 [128, 1024, 256], P(('tx', 'ty'))
- grad_points: bfloat16 [128, 1024, 256], P(('tx', 'ty'))
- grad_w_near: float32 [256, 256], replicated
- grad_gain_one: float32 [256], replicated
- grad_conv: float32 [3, 8, 32, 32], replicated
- grad_gain_two: float32 [256], replicated
- grad_w_up: float32 [256, 1024], replicated
- grad_w_down: float32 [1024, 256], replicated
Inputs may be any that keep to these rules, and one draw needn't show every extreme that they name: `counts`: every tile has at least half of its slots live, and some tile has all of them live. Only live rows count. Among the live rows of one tile at most 16 name the same owner. One particular owner receives exactly 16 live rows from every tile; every other owner receives at most 16 live rows from each tile, so its receive buffer may be partly empty. `zorder`: each owner's entry is a permutation of its 2048 receive slots whose first entries name exactly the filled slots. `border`: each list names distinct live rows of its tile; lists toward a side outside the grid are never read. `near`: indices below 1024 name live rows of the tile; the others name halo rows of blocks whose neighbour tile exists.
All inputs are finite; a program needn't handle non-finite values.
Results may differ from a plain program's by a relative error of at most 0.015.
Values may be sent and summed in bfloat16 or wider, within the bound.
A program may use at most 64 MiB of HBM per device.

v0:
```python
import math
import jax
import jax.numpy as jnp
from jax import lax
from jax.sharding import PartitionSpec as P

PATCH = 1024
eps_norm = 1e-06
gelu_coef = 0.7978845608028654
cubic_coef = 0.044715


def shifted(value, axis, steps):
    count = lax.axis_size(axis)
    initial, last = (max(0, -steps), min(count, count - steps))
    return lax.ppermute(value, axis, [(source, source + steps) for source in range(initial, last)])


def gelu_tanh(value):
    inner = gelu_coef * (value + cubic_coef * value * value * value)
    return 0.5 * value * (1.0 + jnp.tanh(inner))


def gelu_slope(value):
    inner = gelu_coef * (value + cubic_coef * value * value * value)
    tangent = jnp.tanh(inner)
    return 0.5 * (1.0 + tangent) + 0.5 * value * (1.0 - tangent * tangent) * gelu_coef * (
        1.0 + 3.0 * cubic_coef * value * value
    )


def inverse_rms(value):
    return lax.rsqrt(jnp.mean(value * value, axis=-1, keepdims=True) + eps_norm)


def tile_forward(points_tile, halo_rows, near_tile, w_near):
    extended = jnp.concatenate([points_tile, halo_rows], axis=0)
    count_near = near_tile.shape[0]

    def add_neighbour(index, total):
        return total + jnp.take(extended, near_tile[index], axis=0).astype(jnp.float32)

    total = lax.fori_loop(0, count_near, add_neighbour, jnp.zeros(points_tile.shape, jnp.float32))
    average = (total * (1.0 / count_near)).astype(jnp.bfloat16)
    linear_part = jnp.dot(average, w_near, preferred_element_type=jnp.float32)
    lifted = (points_tile.astype(jnp.float32) + gelu_tanh(linear_part)).astype(jnp.bfloat16)
    return (average, linear_part, lifted)


def tile_backward(lifted_grad, average, linear_part, near_tile, w_near, ext_count):
    count_near = near_tile.shape[0]
    tile_rows = lifted_grad.shape[0]
    act_grad = (lifted_grad.astype(jnp.float32) * gelu_slope(linear_part)).astype(jnp.bfloat16)
    near_grad = lax.dot_general(
        average, act_grad, (((0,), (0,)), ((), ())), preferred_element_type=jnp.float32
    )
    spread = lax.dot_general(
        act_grad, w_near, (((1,), (1,)), ((), ())), preferred_element_type=jnp.float32
    ) * (1.0 / count_near)

    def scatter_neighbour(index, total):
        return total.at[near_tile[index]].add(spread)

    ext_grad = lax.fori_loop(
        0, count_near, scatter_neighbour, jnp.zeros((ext_count, spread.shape[1]), jnp.float32)
    )
    row_grad = lifted_grad.astype(jnp.float32) + ext_grad[:tile_rows]
    halo_grad = ext_grad[tile_rows:].astype(jnp.bfloat16)
    return (near_grad, row_grad, halo_grad)


def route_ranks(owner_tile, count, tiles):
    tile_rows = owner_tile.shape[0]
    index = jnp.arange(tile_rows, dtype=jnp.int32)
    live = index < count
    score = jnp.where(live, owner_tile * tile_rows + index, tiles * tile_rows + index)
    order = jnp.argsort(score, stable=True)
    members = (owner_tile[:, None] == jnp.arange(tiles, dtype=jnp.int32)[None, :]) & live[:, None]
    per_owner = jnp.sum(members.astype(jnp.int32), axis=0)
    starts = jnp.cumsum(per_owner) - per_owner
    sorted_owner = jnp.take(owner_tile, order)
    ranked = index - jnp.take(starts, sorted_owner)
    rank = jnp.zeros((tile_rows,), jnp.int32).at[order].set(ranked)
    return (rank, live)


def shift_down(rows):
    return jnp.concatenate([jnp.zeros_like(rows[:1]), rows[:-1]], axis=0)


def shift_up(rows):
    return jnp.concatenate([rows[1:], jnp.zeros_like(rows[:1])], axis=0)


def block_taps(conv_w):
    groups, inner = (conv_w.shape[1], conv_w.shape[2])
    identity_blocks = jnp.eye(groups, dtype=conv_w.dtype)
    full = jnp.einsum("gh,ogab->ogahb", identity_blocks, conv_w)
    return full.reshape(conv_w.shape[0], groups * inner, groups * inner)


def grouped_weight(inputs, outputs, groups, inner):
    length = inputs.shape[0]
    left = inputs.reshape(length, groups, inner)
    right = outputs.reshape(length, groups, inner)
    return jnp.einsum("pga,pgb->gab", left, right, preferred_element_type=jnp.float32)


def tap_back(rows, tap):
    return lax.dot_general(rows, tap, (((1,), (1,)), ((), ())), preferred_element_type=jnp.float32)


def patch_pass(serial, out_grad, gain_one, conv_w, taps_full, gain_two, w_up, w_down):
    groups, inner = (conv_w.shape[1], conv_w.shape[2])
    serial_f = serial.astype(jnp.float32)
    scale_one = inverse_rms(serial_f)
    normed = (serial_f * scale_one * gain_one).astype(jnp.bfloat16)
    taps = (shift_down(normed), normed, shift_up(normed))
    mixed = (
        jnp.dot(taps[0], taps_full[0], preferred_element_type=jnp.float32)
        + jnp.dot(taps[1], taps_full[1], preferred_element_type=jnp.float32)
        + jnp.dot(taps[2], taps_full[2], preferred_element_type=jnp.float32)
    )
    state = serial_f + mixed
    scale_two = inverse_rms(state)
    second = (state * scale_two * gain_two).astype(jnp.bfloat16)
    hidden_pre = jnp.dot(second, w_up, preferred_element_type=jnp.float32)
    hidden = gelu_tanh(hidden_pre).astype(jnp.bfloat16)
    result = (state + jnp.dot(hidden, w_down, preferred_element_type=jnp.float32)).astype(
        jnp.bfloat16
    )
    down_grad = lax.dot_general(
        hidden, out_grad, (((0,), (0,)), ((), ())), preferred_element_type=jnp.float32
    )
    hidden_grad = lax.dot_general(
        out_grad, w_down, (((1,), (1,)), ((), ())), preferred_element_type=jnp.float32
    ).astype(jnp.bfloat16)
    pre_grad = (hidden_grad.astype(jnp.float32) * gelu_slope(hidden_pre)).astype(jnp.bfloat16)
    up_grad = lax.dot_general(
        second, pre_grad, (((0,), (0,)), ((), ())), preferred_element_type=jnp.float32
    )
    second_grad = lax.dot_general(
        pre_grad, w_up, (((1,), (1,)), ((), ())), preferred_element_type=jnp.float32
    ).astype(jnp.bfloat16)
    unit_two = state * scale_two
    weighted_two = second_grad.astype(jnp.float32) * gain_two
    gain_two_grad = jnp.sum(second_grad.astype(jnp.float32) * unit_two, axis=0)
    state_grad = out_grad.astype(jnp.float32) + scale_two * (
        weighted_two - unit_two * jnp.mean(weighted_two * unit_two, axis=-1, keepdims=True)
    )
    mixed_grad = state_grad.astype(jnp.bfloat16)
    conv_grad = jnp.stack(
        [
            grouped_weight(taps[0], mixed_grad, groups, inner),
            grouped_weight(taps[1], mixed_grad, groups, inner),
            grouped_weight(taps[2], mixed_grad, groups, inner),
        ],
        axis=0,
    )
    normed_grad = (
        shift_up(tap_back(mixed_grad, taps_full[0]))
        + tap_back(mixed_grad, taps_full[1])
        + shift_down(tap_back(mixed_grad, taps_full[2]))
    ).astype(jnp.bfloat16)
    unit_one = serial_f * scale_one
    weighted_one = normed_grad.astype(jnp.float32) * gain_one
    gain_one_grad = jnp.sum(normed_grad.astype(jnp.float32) * unit_one, axis=0)
    serial_grad = (
        state_grad
        + scale_one
        * (weighted_one - unit_one * jnp.mean(weighted_one * unit_one, axis=-1, keepdims=True))
    ).astype(jnp.bfloat16)
    return (result, serial_grad, (gain_one_grad, conv_grad, gain_two_grad, up_grad, down_grad))


def pass_columns(rows, shift_by):
    return shifted(rows, "tx", shift_by)


def pass_lines(rows, shift_by):
    return shifted(rows, "ty", shift_by)


def body(
    points,
    counts,
    owner,
    zorder,
    border,
    near,
    w_near,
    gain_one,
    conv_w,
    gain_two,
    w_up,
    w_down,
    grad_out,
):
    points_tile = points[0]
    tile_rows, width = points_tile.shape
    lists = border[0]
    border_rows = lists.shape[1]
    cols_count = lax.axis_size("tx")
    lines_count = lax.axis_size("ty")
    tiles = cols_count * lines_count
    recv_rows = zorder.shape[1]
    capacity = recv_rows // tiles
    near_tile = near[0]
    owner_tile = owner[0]
    sent = jnp.take(points_tile, lists.reshape(-1), axis=0).reshape(4, border_rows, width)
    halo = jnp.concatenate(
        [
            pass_columns(sent[0], -1),
            pass_columns(sent[1], 1),
            pass_lines(sent[2], -1),
            pass_lines(sent[3], 1),
        ],
        axis=0,
    )
    average, linear_part, lifted = tile_forward(points_tile, halo, near_tile, w_near)
    rank, live = route_ranks(owner_tile, counts[0], tiles)
    slots = jnp.where(live, owner_tile * capacity + rank, tiles * capacity)
    payload = jnp.concatenate([lifted, grad_out[0]], axis=1)
    outgoing = (
        jnp.zeros((tiles * capacity, 2 * width), jnp.bfloat16).at[slots].set(payload, mode="drop")
    )
    incoming = lax.all_to_all(outgoing, ("tx", "ty"), split_axis=0, concat_axis=0, tiled=True)
    serial_both = jnp.take(incoming, zorder[0], axis=0)
    taps_full = block_taps(conv_w)
    zero_sums = (
        jnp.zeros((width,), jnp.float32),
        jnp.zeros(conv_w.shape, jnp.float32),
        jnp.zeros((width,), jnp.float32),
        jnp.zeros(w_up.shape, jnp.float32),
        jnp.zeros(w_down.shape, jnp.float32),
    )

    def patch_step(carry, block):
        result, serial_grad, grads = patch_pass(
            block[:, :width], block[:, width:], gain_one, conv_w, taps_full, gain_two, w_up, w_down
        )
        return (jax.tree.map(lambda left, right: left + right, carry, grads), (result, serial_grad))

    sums, (results, serial_grads) = lax.scan(
        patch_step, zero_sums, serial_both.reshape(recv_rows // PATCH, PATCH, 2 * width)
    )
    back = jnp.concatenate(
        [results.reshape(recv_rows, width), serial_grads.reshape(recv_rows, width)], axis=1
    )
    back_slots = jnp.zeros_like(back).at[zorder[0]].set(back)
    returned = lax.all_to_all(back_slots, ("tx", "ty"), split_axis=0, concat_axis=0, tiled=True)
    back_rows = jnp.take(returned, slots, axis=0, mode="fill", fill_value=0)
    out_rows = back_rows[:, :width]
    lifted_grad = back_rows[:, width:]
    near_grad, row_grad, halo_grad = tile_backward(
        lifted_grad, average, linear_part, near_tile, w_near, tile_rows + 4 * border_rows
    )
    came_back = (
        pass_columns(halo_grad[0:border_rows], 1),
        pass_columns(halo_grad[border_rows : 2 * border_rows], -1),
        pass_lines(halo_grad[2 * border_rows : 3 * border_rows], 1),
        pass_lines(halo_grad[3 * border_rows : 4 * border_rows], -1),
    )
    for direction in range(4):
        row_grad = row_grad.at[lists[direction]].add(came_back[direction].astype(jnp.float32))
    near_sum, gain_one_sum, conv_sum, gain_two_sum, up_sum, down_sum = lax.psum(
        (near_grad, sums[0], sums[1], sums[2], sums[3], sums[4]), ("tx", "ty")
    )
    totals = (gain_one_sum, conv_sum, gain_two_sum, up_sum, down_sum)
    scale = 1.0 / math.sqrt(tiles * tile_rows)
    return (
        out_rows[None],
        row_grad.astype(jnp.bfloat16)[None],
        near_sum * scale,
        totals[0] * scale,
        totals[1] * scale,
        totals[2] * scale,
        totals[3] * scale,
        totals[4] * scale,
    )


def solution(mesh):
    placed = (
        P(("tx", "ty"), None, None),
        P(("tx", "ty")),
        P(("tx", "ty"), None),
        P(("tx", "ty"), None),
        P(("tx", "ty"), None, None),
        P(("tx", "ty"), None, None),
        P(),
        P(),
        P(),
        P(),
        P(),
        P(),
        P(("tx", "ty"), None, None),
    )
    return jax.shard_map(
        body,
        mesh=mesh,
        in_specs=placed,
        out_specs=(
            P(("tx", "ty"), None, None),
            P(("tx", "ty"), None, None),
            P(),
            P(),
            P(),
            P(),
            P(),
            P(),
        ),
        check_vma=False,
    )
```

profile of v0, /device:TPU:1, one launch (start us, length us, event | category | flops | bytes accessed | tf_op | source)
XLA Modules:
  0.0 547.0 jit_solution(10170970694803453524)
XLA Ops:
  11.1 4.6 collective-permute-start.3
  24.9 4.4 sort.17
  29.3 4.5 gather_fusion.1
  34.2 6.6 %gather_fusion.2 = s32[1024]{0:T(1024)S(1)} fusion(s32[128]{0:T(128)S(1)} %sub.18, s32[1024]{0:T(1024)S(1)} %broadcast_clamp_fusion.3), kind=kCustom, calls=%fused_computation.2 | custom fusion | bytes 12288 | tf_op jit(solution)/shard_map/jit(_take)/gather | solution.py:82
  40.8 4.3 scatter_custom_fusion.1
  49.6 81.9 %while.51 = (s32[]{:T(128)}, f32[1024,256]{1,0:T(8,128)S(1)}, s32[16,1024]{1,0:T(8,128)}, bf16[1280,256]{1,0:T(8,128)(2,1)S(1)}, s32[]{:T(128)}, /*index=5*/s32[]{:T(128)}) while((s32[]{:T(128)}, f32[1024,256]{1,0:T(8,128)S(1)}, s32[16,1024]{1,0:T(8,128)}, bf16[1280,256]{1,0:T(8,128)(2,1)S(1)}, s32[]{:T(128)}, ...), condition=%wide.region_5.6_spmd.clone, body=%wide.region_4.5_spmd.clone.sunk | while | flops 1058819 | bytes 3700827 | solution.py:43
  55.6 3.9 gather_fusion
  60.7 3.9 gather_fusion
  65.8 3.9 gather_fusion
  70.9 3.9 gather_fusion
  76.0 3.9 gather_fusion
  81.2 3.9 gather_fusion
  86.3 3.9 gather_fusion
  91.4 3.9 gather_fusion
  96.5 3.9 gather_fusion
  101.6 3.9 gather_fusion
  106.7 3.9 gather_fusion
  111.9 3.9 gather_fusion
  133.7 6.7 %scatter_custom_fusion.2 = bf16[2048,512]{1,0:T(8,128)(2,1)} fusion(s32[1024]{0:T(1024)S(1)} %get-tuple-element.408, bf16[1024,512]{1,0:T(8,128)(2,1)S(1)} %copy.65, bf16[]{:T(256)} %constant.215.clone.1), kind=kCustom, calls=%fused_computation.126 | custom fusion | bytes 2097154 | tf_op jit(solution)/shard_map/scatter | solution.py:225
  140.4 22.0 %all-to-all-start = ((bf16[128,16,512]{2,1,0:T(8,128)(2,1)}), bf16[128,16,512]{2,1,0:T(8,128)(2,1)S(1)}, u32[]{:S(2)}, u32[]{:S(2)}) async-start(bf16[128,16,512]{2,1,0:T(8,128)(2,1)} %bitcast.194), calls=%async_computation | async-start | bytes 4194304 | tf_op jit(solution)/shard_map/all_to_all | solution.py:227
  169.1 23.7 %all-to-all-done = bf16[128,16,512]{2,1,0:T(8,128)(2,1)S(1)} async-done(((bf16[128,16,512]{2,1,0:T(8,128)(2,1)}), bf16[128,16,512]{2,1,0:T(8,128)(2,1)S(1)}, u32[]{:S(2)}, u32[]{:S(2)}) %all-to-all-start) | async-done | bytes 2097184 | tf_op jit(solution)/shard_map/all_to_all | solution.py:227
  192.8 9.2 %gather_fusion.4 = bf16[2048,512]{1,0:T(8,128)(2,1)} fusion(bf16[2048,512]{1,0:T(8,128)(2,1)S(1)} %bitcast.188, s32[2048]{0:T(1024)S(1)} %broadcast_clamp_fusion.1), kind=kCustom, calls=%fused_computation.4 | custom fusion | bytes 4202496 | tf_op jit(solution)/shard_map/jit(_take)/gather | solution.py:228
  206.6 68.3 %while.52 = (s32[]{:T(128)}, f32[256]{0:T(256)S(1)}, f32[3,8,32,32]{3,2,1,0:T(8,128)}, f32[256]{0:T(256)S(1)}, f32[256,1024]{1,0:T(8,128)}, /*index=5*/f32[1024,...) while((s32[]{:T(128)}, f32[256]{0:T(256)S(1)}, ...), condition=%wide.region_14.15_spmd.clone, body=%wide.region_7.14_spmd.clone.sunk | while | flops 4135946752 | bytes 123703776 | solution.py:244
  221.8 4.9 convolution_add_fusion.11
  255.8 5.2 convolution_add_fusion.11
  274.9 11.5 %scatter_custom_fusion.3 = bf16[2048,512]{1,0:T(8,128)(2,1)} fusion(s32[2048]{0:T(1024)} %bitcast.205, bf16[2048,256]{1,0:T(8,128)(2,1)} %bitcast.198, bf16[]{:T(256)} %constant.244, bf16[2048,256]{1,0:T(8,128)(2,1)} %bitcast.199, bf16[]{:T(256)} %constant.215.clone.1), kind=kCustom, calls=%fused_computation.105 | custom fusion | flops 4194304 | bytes 4195328 | tf_op jit(solution)/shard_map/scatter | solution.py:250
  286.4 4.3 all-to-all-start.1
  291.3 81.3 %all-reduce.4 = (f32[256]{0:T(256)S(1)}, f32[256]{0:T(256)S(1)}) all-reduce(f32[256]{0:T(256)S(1)} %get-tuple-element.250, f32[256]{0:T(256)S(1)} %get-tuple-element.252), channel_id=1, replica_groups=mesh['tx'=4,'ty'=32] {'tx','ty'}, use_global_device_ids=true, to_apply=%region_24.25 | all-reduce | flops 512 | bytes 4096 | tf_op jit(solution)/shard_map/psum | solution.py:266
  373.2 4.0 gather_fusion.5
  381.2 117.5 %while.50 = (s32[]{:T(128)}, f32[1280,256]{1,0:T(8,128)S(1)}, s32[16,1024]{1,0:T(8,128)}, f32[1024,256]{1,0:T(8,128)S(1)}, s32[]{:T(128)}) while((s32[]{:T(128)}, f32[1280,256]{1,0:T(8,128)S(1)}, s32[16,1024]{1,0:T(8,128)}, f32[1024,256]{1,0:T(8,128)S(1)}, s32[]{:T(128)}) %tuple.124), condition=%wide.region_18.19_spmd, body=%wide.region_16.18_spmd.sunk | while | flops 265218 | bytes 3158089 | solution.py:64
  382.0 6.5 %scatter_fusion = f32[1280,256]{1,0:T(8,128)S(1)} fusion(f32[1280,256]{1,0:T(8,128)S(1)} %get-tuple-element.679, s32[1024]{0:T(1024)S(1)} %bitcast.200, f32[1024,256]{1,0:T(8,128)S(1)} %get-tuple-element.686), kind=kCustom, calls=%fused_computation.6.clone.1 | custom fusion | flops 262144 | bytes 3149824 | tf_op jit(solution)/shard_map/while/body/eval_jaxpr/scatter-add | solution.py:62
  389.4 6.5 %scatter_fusion = f32[1280,256]{1,0:T(8,128)S(1)} fusion(f32[1280,256]{1,0:T(8,128)S(1)} %get-tuple-element.679, s32[1024]{0:T(1024)S(1)} %bitcast.200, f32[1024,256]{1,0:T(8,128)S(1)} %get-tuple-element.686), kind=kCustom, calls=%fused_computation.6.clone.1 | custom fusion | flops 262144 | bytes 3149824 | tf_op jit(solution)/shard_map/while/body/eval_jaxpr/scatter-add | solution.py:62
  396.7 6.5 %scatter_fusion = f32[1280,256]{1,0:T(8,128)S(1)} fusion(f32[1280,256]{1,0:T(8,128)S(1)} %get-tuple-element.679, s32[1024]{0:T(1024)S(1)} %bitcast.200, f32[1024,256]{1,0:T(8,128)S(1)} %get-tuple-element.686), kind=kCustom, calls=%fused_computation.6.clone.1 | custom fusion | flops 262144 | bytes 3149824 | tf_op jit(solution)/shard_map/while/body/eval_jaxpr/scatter-add | solution.py:62
  404.1 6.5 %scatter_fusion = f32[1280,256]{1,0:T(8,128)S(1)} fusion(f32[1280,256]{1,0:T(8,128)S(1)} %get-tuple-element.679, s32[1024]{0:T(1024)S(1)} %bitcast.200, f32[1024,256]{1,0:T(8,128)S(1)} %get-tuple-element.686), kind=kCustom, calls=%fused_computation.6.clone.1 | custom fusion | flops 262144 | bytes 3149824 | tf_op jit(solution)/shard_map/while/body/eval_jaxpr/scatter-add | solution.py:62
  411.4 6.5 %scatter_fusion = f32[1280,256]{1,0:T(8,128)S(1)} fusion(f32[1280,256]{1,0:T(8,128)S(1)} %get-tuple-element.679, s32[1024]{0:T(1024)S(1)} %bitcast.200, f32[1024,256]{1,0:T(8,128)S(1)} %get-tuple-element.686), kind=kCustom, calls=%fused_computation.6.clone.1 | custom fusion | flops 262144 | bytes 3149824 | tf_op jit(solution)/shard_map/while/body/eval_jaxpr/scatter-add | solution.py:62
  418.7 6.5 %scatter_fusion = f32[1280,256]{1,0:T(8,128)S(1)} fusion(f32[1280,256]{1,0:T(8,128)S(1)} %get-tuple-element.679, s32[1024]{0:T(1024)S(1)} %bitcast.200, f32[1024,256]{1,0:T(8,128)S(1)} %get-tuple-element.686), kind=kCustom, calls=%fused_computation.6.clone.1 | custom fusion | flops 262144 | bytes 3149824 | tf_op jit(solution)/shard_map/while/body/eval_jaxpr/scatter-add | solution.py:62
  426.1 6.5 %scatter_fusion = f32[1280,256]{1,0:T(8,128)S(1)} fusion(f32[1280,256]{1,0:T(8,128)S(1)} %get-tuple-element.679, s32[1024]{0:T(1024)S(1)} %bitcast.200, f32[1024,256]{1,0:T(8,128)S(1)} %get-tuple-element.686), kind=kCustom, calls=%fused_computation.6.clone.1 | custom fusion | flops 262144 | bytes 3149824 | tf_op jit(solution)/shard_map/while/body/eval_jaxpr/scatter-add | solution.py:62
  433.4 6.5 %scatter_fusion = f32[1280,256]{1,0:T(8,128)S(1)} fusion(f32[1280,256]{1,0:T(8,128)S(1)} %get-tuple-element.679, s32[1024]{0:T(1024)S(1)} %bitcast.200, f32[1024,256]{1,0:T(8,128)S(1)} %get-tuple-element.686), kind=kCustom, calls=%fused_computation.6.clone.1 | custom fusion | flops 262144 | bytes 3149824 | tf_op jit(solution)/shard_map/while/body/eval_jaxpr/scatter-add | solution.py:62
  440.8 6.5 %scatter_fusion = f32[1280,256]{1,0:T(8,128)S(1)} fusion(f32[1280,256]{1,0:T(8,128)S(1)} %get-tuple-element.679, s32[1024]{0:T(1024)S(1)} %bitcast.200, f32[1024,256]{1,0:T(8,128)S(1)} %get-tuple-element.686), kind=kCustom, calls=%fused_computation.6.clone.1 | custom fusion | flops 262144 | bytes 3149824 | tf_op jit(solution)/shard_map/while/body/eval_jaxpr/scatter-add | solution.py:62
  448.1 6.5 %scatter_fusion = f32[1280,256]{1,0:T(8,128)S(1)} fusion(f32[1280,256]{1,0:T(8,128)S(1)} %get-tuple-element.679, s32[1024]{0:T(1024)S(1)} %bitcast.200, f32[1024,256]{1,0:T(8,128)S(1)} %get-tuple-element.686), kind=kCustom, calls=%fused_computation.6.clone.1 | custom fusion | flops 262144 | bytes 3149824 | tf_op jit(solution)/shard_map/while/body/eval_jaxpr/scatter-add | solution.py:62
  455.5 6.5 %scatter_fusion = f32[1280,256]{1,0:T(8,128)S(1)} fusion(f32[1280,256]{1,0:T(8,128)S(1)} %get-tuple-element.679, s32[1024]{0:T(1024)S(1)} %bitcast.200, f32[1024,256]{1,0:T(8,128)S(1)} %get-tuple-element.686), kind=kCustom, calls=%fused_computation.6.clone.1 | custom fusion | flops 262144 | bytes 3149824 | tf_op jit(solution)/shard_map/while/body/eval_jaxpr/scatter-add | solution.py:62
  462.8 6.5 %scatter_fusion = f32[1280,256]{1,0:T(8,128)S(1)} fusion(f32[1280,256]{1,0:T(8,128)S(1)} %get-tuple-element.679, s32[1024]{0:T(1024)S(1)} %bitcast.200, f32[1024,256]{1,0:T(8,128)S(1)} %get-tuple-element.686), kind=kCustom, calls=%fused_computation.6.clone.1 | custom fusion | flops 262144 | bytes 3149824 | tf_op jit(solution)/shard_map/while/body/eval_jaxpr/scatter-add | solution.py:62
  470.1 6.5 %scatter_fusion = f32[1280,256]{1,0:T(8,128)S(1)} fusion(f32[1280,256]{1,0:T(8,128)S(1)} %get-tuple-element.679, s32[1024]{0:T(1024)S(1)} %bitcast.200, f32[1024,256]{1,0:T(8,128)S(1)} %get-tuple-element.686), kind=kCustom, calls=%fused_computation.6.clone.1 | custom fusion | flops 262144 | bytes 3149824 | tf_op jit(solution)/shard_map/while/body/eval_jaxpr/scatter-add | solution.py:62
  477.5 6.5 %scatter_fusion = f32[1280,256]{1,0:T(8,128)S(1)} fusion(f32[1280,256]{1,0:T(8,128)S(1)} %get-tuple-element.679, s32[1024]{0:T(1024)S(1)} %bitcast.200, f32[1024,256]{1,0:T(8,128)S(1)} %get-tuple-element.686), kind=kCustom, calls=%fused_computation.6.clone.1 | custom fusion | flops 262144 | bytes 3149824 | tf_op jit(solution)/shard_map/while/body/eval_jaxpr/scatter-add | solution.py:62
  484.8 6.5 %scatter_fusion = f32[1280,256]{1,0:T(8,128)S(1)} fusion(f32[1280,256]{1,0:T(8,128)S(1)} %get-tuple-element.679, s32[1024]{0:T(1024)S(1)} %bitcast.200, f32[1024,256]{1,0:T(8,128)S(1)} %get-tuple-element.686), kind=kCustom, calls=%fused_computation.6.clone.1 | custom fusion | flops 262144 | bytes 3149824 | tf_op jit(solution)/shard_map/while/body/eval_jaxpr/scatter-add | solution.py:62
  492.2 6.5 %scatter_fusion = f32[1280,256]{1,0:T(8,128)S(1)} fusion(f32[1280,256]{1,0:T(8,128)S(1)} %get-tuple-element.679, s32[1024]{0:T(1024)S(1)} %bitcast.200, f32[1024,256]{1,0:T(8,128)S(1)} %get-tuple-element.686), kind=kCustom, calls=%fused_computation.6.clone.1 | custom fusion | flops 262144 | bytes 3149824 | tf_op jit(solution)/shard_map/while/body/eval_jaxpr/scatter-add | solution.py:62
  507.5 4.0 collective-permute-start.4
  520.6 11.0 %all-reduce.8.cloned.1.call-done = (f32[256,256]{1,0:T(8,128)}, f32[3,8,32,32]{3,2,1,0:T(8,128)}, f32[256,1024]{1,0:T(8,128)}, f32[1024,256]{1,0:T(8,128)}) async-done(((f32[256,256]{1,0:T(8,128)}, f32[3,8,32,32]{3,2,1,0:T(8,128)}, f32[256,1024]{1,0:T(8,128)}, f32[1024,256]{1,0:T(8,128)}), (f32[256,256]{1,0:T(8,128)}, f32[3,8,32,32]{3,2,1,0:T(8,128)}, f32[256,1024]{1,0:T(8,128)}, ...) | async-done | bytes 2457616 | tf_op jit(solution)/shard_map/psum | solution.py:266
  (313 shorter events, 165.5 us)
Async XLA Ops:
  7.2 124.4 %copy-start = (bf16[256,256]{1,0:T(8,128)(2,1)S(1)}, bf16[256,256]{1,0:T(8,128)(2,1)}, u32[]{:S(2)}) copy-start(bf16[256,256]{1,0:T(8,128)(2,1)} %param.25) | copy-start | bytes 393220
  7.2 22.1 %copy-start.1 = (s32[1,1024]{1,0:T(1,128)S(1)}, s32[1,1024]{1,0:T(1,128)}, u32[]{:S(2)}) copy-start(s32[1,1024]{1,0:T(1,128)} %param.21) | copy-start | bytes 12292
  11.1 35.9 %collective-permute-start.3 = (bf16[64,256]{0,1:T(8,128)(2,1)S(1)}, bf16[64,256]{0,1:T(8,128)(2,1)S(1)}, u32[]{:S(2)}, u32[]{:S(2)}) collective-permute-start(bf16[64,256]{0,1:T(8,128)(2,1)S(1)} %get-tuple-element.423), channel_id=1, source_target_pairs={{0,1},{1,2},{2,3},{3,4},{4,5},{5,6},{6,7},{7,8},{8,9},{9,10},{10,1... | collective-permute-start | bytes 98312 | tf_op jit(solution)/shard_map/ppermute | solution.py:16
  15.7 31.3 %collective-permute-start.2 = (bf16[64,256]{0,1:T(8,128)(2,1)S(1)}, bf16[64,256]{0,1:T(8,128)(2,1)S(1)}, u32[]{:S(2)}, u32[]{:S(2)}) collective-permute-start(bf16[64,256]{0,1:T(8,128)(2,1)S(1)} %get-tuple-element.424), channel_id=1, source_target_pairs={{1,0},{2,1},{3,2},{4,3},{5,4},{6,5},{7,6},{8,7},{9,8},{10,9},{11,1... | collective-permute-start | bytes 98312 | tf_op jit(solution)/shard_map/ppermute | solution.py:16
  17.6 29.4 %collective-permute-start.1 = (bf16[64,256]{0,1:T(8,128)(2,1)S(1)}, bf16[64,256]{0,1:T(8,128)(2,1)S(1)}, u32[]{:S(2)}, u32[]{:S(2)}) collective-permute-start(bf16[64,256]{0,1:T(8,128)(2,1)S(1)} %get-tuple-element.425), channel_id=1, source_target_pairs={{0,32},{32,64},{64,96},{1,33},{33,65},{65,97},{2,34},{34,66},{66,9... | collective-permute-start | bytes 98312 | tf_op jit(solution)/shard_map/ppermute | solution.py:16
  21.2 25.8 %collective-permute-start = (bf16[64,256]{0,1:T(8,128)(2,1)S(1)}, bf16[64,256]{0,1:T(8,128)(2,1)S(1)}, u32[]{:S(2)}, u32[]{:S(2)}) collective-permute-start(bf16[64,256]{0,1:T(8,128)(2,1)S(1)} %get-tuple-element.426), channel_id=1, source_target_pairs={{32,0},{64,32},{96,64},{33,1},{65,33},{97,65},{34,2},{66,34},{98,6... | collective-permute-start | bytes 98312 | tf_op jit(solution)/shard_map/ppermute | solution.py:16
  29.3 16.5 %copy-start.12 = (bf16[1,1024,256]{2,1,0:T(8,128)(2,1)S(1)}, bf16[1,1024,256]{2,1,0:T(8,128)(2,1)}, u32[]{:S(2)}) copy-start(bf16[1,1024,256]{2,1,0:T(8,128)(2,1)} %param.19) | copy-start | bytes 1572868
  29.3 16.7 %copy-start.14 = (bf16[1,1024,256]{2,1,0:T(8,128)(2,1)S(1)}, bf16[1,1024,256]{2,1,0:T(8,128)(2,1)}, u32[]{:S(2)}) copy-start(bf16[1,1024,256]{2,1,0:T(8,128)(2,1)} %param.31) | copy-start | bytes 1572868
  45.7 87.9 %copy-start.24 = (s32[1024]{0:T(1024)}, s32[1024]{0:T(1024)S(1)}, u32[]{:S(2)}) copy-start(s32[1024]{0:T(1024)S(1)} %get-tuple-element.408) | copy-start | bytes 12292
  47.0 0.6 copy-start.18
  47.0 0.6 copy-start.19
  49.6 83.5 %copy-start.13 = (bf16[1,1024,256]{1,2,0:T(8,128)(2,1)S(1)}, bf16[1,1024,256]{1,2,0:T(8,128)(2,1)}, u32[]{:S(2)}) copy-start(bf16[1,1024,256]{1,2,0:T(8,128)(2,1)} %copy.64) | copy-start | bytes 1572868
  131.5 8.9 %copy-start.6 = (f32[1024,256]{1,0:T(8,128)}, f32[1024,256]{1,0:T(8,128)S(1)}, u32[]{:S(2)}) copy-start(f32[1024,256]{1,0:T(8,128)S(1)} %get-tuple-element.246) | copy-start | bytes 3145732
  133.1 29.9 %copy-start.21 = (s32[1,2048]{1,0:T(1,128)S(1)}, s32[1,2048]{1,0:T(1,128)}, u32[]{:S(2)}) copy-start(s32[1,2048]{1,0:T(1,128)} %param.22) | copy-start | bytes 24580
  140.4 52.4 %all-to-all-start = ((bf16[128,16,512]{2,1,0:T(8,128)(2,1)}), bf16[128,16,512]{2,1,0:T(8,128)(2,1)S(1)}, u32[]{:S(2)}, u32[]{:S(2)}) async-start(bf16[128,16,512]{2,1,0:T(8,128)(2,1)} %bitcast.194), calls=%async_computation | async-start | bytes 4194304 | tf_op jit(solution)/shard_map/all_to_all | solution.py:227
  169.1 32.9 %copy-start.22 = (s32[2048,1]{0,1:T(1,128)}, s32[2048,1]{0,1:T(1,128)S(1)}, u32[]{:S(2)}) copy-start(s32[2048,1]{0,1:T(1,128)S(1)} %compare_select_fusion.3) | copy-start | bytes 24580
  202.0 4.6 copy-start.15
  202.0 4.6 copy-start.16
  213.4 4.7 copy-start.27
  216.1 1.9 copy-start.2
  221.8 4.9 copy-start.3
  221.8 4.9 copy-start.28
  229.8 2.1 copy-start.8
  231.9 1.3 copy-start.4
  231.9 1.9 copy-start.5
  232.8 3.0 copy-start.9
  232.8 1.3 copy-start.10
  234.3 4.3 copy-start.11
  247.4 4.7 copy-start.27
  250.1 1.9 copy-start.2
  255.8 5.2 copy-start.3
  255.8 5.2 copy-start.28
  264.1 2.1 copy-start.8
  266.2 1.3 copy-start.4
  266.2 1.9 copy-start.5
  267.1 3.0 copy-start.9
  267.1 1.3 copy-start.10
  268.6 4.3 copy-start.11
  274.9 15.9 %copy-start.23 = (s32[1,4,64]{2,1,0:T(4,128)S(1)}, s32[1,4,64]{2,1,0:T(4,128)}, u32[]{:S(2)}) copy-start(s32[1,4,64]{2,1,0:T(4,128)} %param.23) | copy-start | bytes 3076
  274.9 16.4 %copy-start.25 = (s32[1024]{0:T(1024)S(1)}, s32[1024]{0:T(1024)}, u32[]{:S(2)}) copy-start(s32[1024]{0:T(1024)} %copy-done.24) | copy-start | bytes 12292
  286.4 86.8 %all-to-all-start.1 = ((bf16[128,16,512]{2,1,0:T(8,128)(2,1)}), bf16[128,16,512]{2,1,0:T(8,128)(2,1)S(1)}, u32[]{:S(2)}, u32[]{:S(2)}) async-start(bf16[128,16,512]{2,1,0:T(8,128)(2,1)} %bitcast.193), calls=%async_computation.1 | async-start | bytes 4194304 | tf_op jit(solution)/shard_map/all_to_all | solution.py:251
  290.7 240.9 %all-reduce.8.cloned.1.call-start = ((), (), s32[]{:S(2)}) async-start(), calls=%async_computation.2 | async-start | bytes 5505024 | tf_op jit(solution)/shard_map/psum | solution.py:266
  373.2 4.5 copy-start.26
  377.1 2.6 copy-start.7
  500.3 18.1 %collective-permute-start.7 = (bf16[64,256]{1,0:T(8,128)(2,1)S(1)}, bf16[64,256]{1,0:T(8,128)(2,1)S(1)}, u32[]{:S(2)}, u32[]{:S(2)}) collective-permute-start(bf16[64,256]{1,0:T(8,128)(2,1)S(1)} %get-tuple-element.419), channel_id=1, source_target_pairs={{1,0},{2,1},{3,2},{4,3},{5,4},{6,5},{7,6},{8,7},{9,8},{10,9},{11,1... | collective-permute-start | bytes 98312 | tf_op jit(solution)/shard_map/ppermute | solution.py:16
  502.8 14.3 %collective-permute-start.6 = (bf16[64,256]{1,0:T(8,128)(2,1)S(1)}, bf16[64,256]{1,0:T(8,128)(2,1)S(1)}, u32[]{:S(2)}, u32[]{:S(2)}) collective-permute-start(bf16[64,256]{1,0:T(8,128)(2,1)S(1)} %get-tuple-element.420), channel_id=1, source_target_pairs={{0,1},{1,2},{2,3},{3,4},{4,5},{5,6},{6,7},{7,8},{8,9},{9,10},{10,1... | collective-permute-start | bytes 98312 | tf_op jit(solution)/shard_map/ppermute | solution.py:16
  506.2 9.6 %collective-permute-start.5 = (bf16[64,256]{1,0:T(8,128)(2,1)S(1)}, bf16[64,256]{1,0:T(8,128)(2,1)S(1)}, u32[]{:S(2)}, u32[]{:S(2)}) collective-permute-start(bf16[64,256]{1,0:T(8,128)(2,1)S(1)} %get-tuple-element.421), channel_id=1, source_target_pairs={{32,0},{64,32},{96,64},{33,1},{65,33},{97,65},{34,2},{66,34},{98,6... | collective-permute-start | bytes 98312 | tf_op jit(solution)/shard_map/ppermute | solution.py:16
  507.5 6.8 %collective-permute-start.4 = (bf16[64,256]{1,0:T(8,128)(2,1)S(1)}, bf16[64,256]{1,0:T(8,128)(2,1)S(1)}, u32[]{:S(2)}, u32[]{:S(2)}) collective-permute-start(bf16[64,256]{1,0:T(8,128)(2,1)S(1)} %get-tuple-element.422), channel_id=1, source_target_pairs={{0,32},{32,64},{64,96},{1,33},{33,65},{65,97},{2,34},{34,66},{66,9... | collective-permute-start | bytes 98312 | tf_op jit(solution)/shard_map/ppermute | solution.py:16
  (2 other events, 1.3 us)
Sparse Core Ops, SparseCore 0:
  381.3 150.3 all-reduce.7
where the time goes:
time: 558 us; the launch traced here: 547 us
  other arithmetic  180 us (32%)
  local copies, waits for them, and re-layouts  133 us (24%)
  blocking collectives  81.3 us (15%)
  matrix products  51.8 us (9%)
  starting transfers between devices  48.9 us (9%)
  waiting for transfers between devices  34.8 us (6%)
  between operations  15.7 us (3%)
    scatter-add x16, other arithmetic, scatter_neighbour(): return total.at[near_tile[index]].add(spread)  105 us
    psum x1, blocking collectives, body(): lax.psum((near_grad, sums[0], sums[1], sums[2], sums[3], sums[4]), ('tx',...  81.3 us
    gather x16, local copies, waits for them, and re-layouts, add_neighbour(): jnp.take(extended, near_tile[index], axis=0).astype(jnp.float32)  63.1 us
    all_to_all x1, waiting for transfers between devices, body(): lax.all_to_all(outgoing, ('tx', 'ty'), split_axis=0, concat_axis=0, tiled...  23.7 us
    ppermute x8, starting transfers between devices, shifted(): lax.ppermute(value, axis, [(source, source + steps) for source in range(i...  22.5 us
    all_to_all x1, starting transfers between devices, body(): lax.all_to_all(outgoing, ('tx', 'ty'), split_axis=0, concat_axis=0, tiled...  22 us
    select_n x16, other arithmetic, add_neighbour(): jnp.take(extended, near_tile[index], axis=0).astype(jnp.float32)  12.4 us
    select_n x16, other arithmetic, scatter_neighbour(): return total.at[near_tile[index]].add(spread)  12.3 us
  transfers between devices with their start and end apart: 11, of which 2 were waited for; matrix products, arithmetic and copies ran while one was open for 29% of the time, Pallas kernels for 0%

commit v1 on v0

--- a/solution.py
+++ b/solution.py
@@ -3,6 +3,7 @@
 import jax.numpy as jnp
 from jax import lax
 from jax.sharding import PartitionSpec as P
+from jax.lax import psum
 
 PATCH = 1024
 eps_norm = 1e-06
@@ -263,8 +264,9 @@
     )
     for direction in range(4):
         row_grad = row_grad.at[lists[direction]].add(came_back[direction].astype(jnp.float32))
-    near_sum, gain_one_sum, conv_sum, gain_two_sum, up_sum, down_sum = lax.psum(
-        (near_grad, sums[0], sums[1], sums[2], sums[3], sums[4]), ("tx", "ty")
+    near_sum, gain_one_sum, conv_sum, gain_two_sum, up_sum, down_sum = psum(
+        psum((near_grad, sums[0], sums[1], sums[2], sums[3], sums[4]), axis_name="ty"),
+        axis_name="tx",
     )
     totals = (gain_one_sum, conv_sum, gain_two_sum, up_sum, down_sum)
     scale = 1.0 / math.sqrt(tiles * tile_rows)

time: 558 us -> 599 us (1.073)
  waiting for transfers between devices: 34.8 us -> 85.6 us
  blocking collectives: 81.3 us -> 70.1 us
    all_to_all x1, waiting for transfers between devices: 0.01 us -> 30.6 us  [body(): lax.all_to_all(back_slots, ('tx', 'ty'), split_axis=0, concat_axis=0, til...]
    psum x1 -> x2, waiting for transfers between devices: 11 us -> 31.2 us  [the longest x1 31.2 us: body(): psum((near_grad, sums[0], sums[1], sums[2], sums[3], sums[4]), axis_name=...]
    psum x1 -> x2, blocking collectives: 81.3 us -> 70.1 us  [the longest x1 63.3 us: body(): psum((near_grad, sums[0], sums[1], sums[2], sums[3], sums[4]), axis_name=...]
  transfers between devices with their start and end apart: 11 -> 12, of which waited for: 2 -> 3; matrix products, arithmetic and copies ran while one was open for 29% -> 27% of each run, Pallas kernels for 0% -> 0%
where the time goes in v1:
time: 599 us; the launch traced here: 588 us
  other arithmetic  180 us (30%)
  local copies, waits for them, and re-layouts  133 us (22%)
  waiting for transfers between devices  85.6 us (14%)
  blocking collectives  70.1 us (12%)
  matrix products  52.8 us (9%)
  starting transfers between devices  48.6 us (8%)
  between operations  15.7 us (3%)
    scatter-add x16, other arithmetic, scatter_neighbour(): return total.at[near_tile[index]].add(spread)  105 us
    psum x1, blocking collectives, body(): psum((near_grad, sums[0], sums[1], sums[2], sums[3], sums[4]), axis_name=...  63.3 us
    gather x16, local copies, waits for them, and re-layouts, add_neighbour(): jnp.take(extended, near_tile[index], axis=0).astype(jnp.float32)  63.1 us
    psum x1, waiting for transfers between devices, body(): psum((near_grad, sums[0], sums[1], sums[2], sums[3], sums[4]), axis_name=...  31.2 us
    all_to_all x1, waiting for transfers between devices, body(): lax.all_to_all(back_slots, ('tx', 'ty'), split_axis=0, concat_axis=0, til...  30.6 us
    all_to_all x1, waiting for transfers between devices, body(): lax.all_to_all(outgoing, ('tx', 'ty'), split_axis=0, concat_axis=0, tiled...  23.8 us
    ppermute x8, starting transfers between devices, shifted(): lax.ppermute(value, axis, [(source, source + steps) for source in range(i...  22.2 us
    all_to_all x1, starting transfers between devices, body(): lax.all_to_all(outgoing, ('tx', 'ty'), split_axis=0, concat_axis=0, tiled...  22 us
  transfers between devices with their start and end apart: 12, of which 3 were waited for; matrix products, arithmetic and copies ran while one was open for 27% of the time, Pallas kernels for 0%

profile of v1, /device:TPU:1, one launch (start us, length us, event | category | flops | bytes accessed | tf_op | source)
XLA Modules:
  0.0 587.7 jit_solution(15298942087728561983)
XLA Ops:
  11.1 4.6 collective-permute-start.3
  24.9 4.4 sort.17
  29.3 4.5 gather_fusion.1
  34.2 6.6 %gather_fusion.2 = s32[1024]{0:T(1024)S(1)} fusion(s32[128]{0:T(128)S(1)} %sub.18, s32[1024]{0:T(1024)S(1)} %broadcast_clamp_fusion.3), kind=kCustom, calls=%fused_computation.2 | custom fusion | bytes 12288 | tf_op jit(solution)/shard_map/jit(_take)/gather | solution.py:83
  40.8 4.3 scatter_custom_fusion.1
  49.6 81.9 %while.51 = (s32[]{:T(128)}, f32[1024,256]{1,0:T(8,128)S(1)}, s32[16,1024]{1,0:T(8,128)}, bf16[1280,256]{1,0:T(8,128)(2,1)S(1)}, s32[]{:T(128)}, /*index=5*/s32[]{:T(128)}) while((s32[]{:T(128)}, f32[1024,256]{1,0:T(8,128)S(1)}, s32[16,1024]{1,0:T(8,128)}, bf16[1280,256]{1,0:T(8,128)(2,1)S(1)}, s32[]{:T(128)}, ...), condition=%wide.region_5.6_spmd.clone, body=%wide.region_4.5_spmd.clone.sunk | while | flops 1058819 | bytes 3700827 | solution.py:44
  50.5 3.9 gather_fusion
  55.6 3.9 gather_fusion
  60.7 3.9 gather_fusion
  65.8 3.9 gather_fusion
  70.9 3.9 gather_fusion
  76.0 3.9 gather_fusion
  81.1 3.9 gather_fusion
  86.3 3.9 gather_fusion
  91.4 3.9 gather_fusion
  96.5 3.9 gather_fusion
  133.7 6.7 %scatter_custom_fusion.2 = bf16[2048,512]{1,0:T(8,128)(2,1)} fusion(s32[1024]{0:T(1024)S(1)} %get-tuple-element.414, bf16[1024,512]{1,0:T(8,128)(2,1)S(1)} %copy.65, bf16[]{:T(256)} %constant.215.clone.1), kind=kCustom, calls=%fused_computation.126 | custom fusion | bytes 2097154 | tf_op jit(solution)/shard_map/scatter | solution.py:226
  140.4 22.0 %all-to-all-start = ((bf16[128,16,512]{2,1,0:T(8,128)(2,1)}), bf16[128,16,512]{2,1,0:T(8,128)(2,1)S(1)}, u32[]{:S(2)}, u32[]{:S(2)}) async-start(bf16[128,16,512]{2,1,0:T(8,128)(2,1)} %bitcast.194), calls=%async_computation | async-start | bytes 4194304 | tf_op jit(solution)/shard_map/all_to_all | solution.py:228
  169.1 23.8 %all-to-all-done = bf16[128,16,512]{2,1,0:T(8,128)(2,1)S(1)} async-done(((bf16[128,16,512]{2,1,0:T(8,128)(2,1)}), bf16[128,16,512]{2,1,0:T(8,128)(2,1)S(1)}, u32[]{:S(2)}, u32[]{:S(2)}) %all-to-all-start) | async-done | bytes 2097184 | tf_op jit(solution)/shard_map/all_to_all | solution.py:228
  192.8 9.2 %gather_fusion.4 = bf16[2048,512]{1,0:T(8,128)(2,1)} fusion(bf16[2048,512]{1,0:T(8,128)(2,1)S(1)} %bitcast.188, s32[2048]{0:T(1024)S(1)} %broadcast_clamp_fusion.1), kind=kCustom, calls=%fused_computation.4 | custom fusion | bytes 4202496 | tf_op jit(solution)/shard_map/jit(_take)/gather | solution.py:229
  206.6 68.3 %while.52 = (s32[]{:T(128)}, f32[256]{0:T(256)S(1)}, f32[3,8,32,32]{3,2,1,0:T(8,128)}, f32[256]{0:T(256)S(1)}, f32[256,1024]{1,0:T(8,128)}, /*index=5*/f32[1024,...) while((s32[]{:T(128)}, f32[256]{0:T(256)S(1)}, ...), condition=%wide.region_14.15_spmd.clone, body=%wide.region_7.14_spmd.clone.sunk | while | flops 4135946752 | bytes 123703776 | solution.py:245
  221.9 4.9 convolution_add_fusion.11
  255.9 5.2 convolution_add_fusion.11
  274.9 11.5 %scatter_custom_fusion.3 = bf16[2048,512]{1,0:T(8,128)(2,1)} fusion(s32[2048]{0:T(1024)} %bitcast.205, bf16[2048,256]{1,0:T(8,128)(2,1)} %bitcast.198, bf16[]{:T(256)} %constant.244, bf16[2048,256]{1,0:T(8,128)(2,1)} %bitcast.199, bf16[]{:T(256)} %constant.215.clone.1), kind=kCustom, calls=%fused_computation.105 | custom fusion | flops 4194304 | bytes 4195328 | tf_op jit(solution)/shard_map/scatter | solution.py:251
  286.4 4.4 all-to-all-start.1
  290.8 30.6 %all-to-all-done.1 = bf16[128,16,512]{2,1,0:T(8,128)(2,1)S(1)} async-done(((bf16[128,16,512]{2,1,0:T(8,128)(2,1)}), bf16[128,16,512]{2,1,0:T(8,128)(2,1)S(1)}, u32[]{:S(2)}, u32[]{:S(2)}) %all-to-all-start.1) | async-done | bytes 2097184 | tf_op jit(solution)/shard_map/all_to_all | solution.py:252
  321.4 4.0 gather_fusion.5
  329.7 63.3 %all-reduce.4 = (f32[256]{0:T(256)S(1)}, f32[256]{0:T(256)S(1)}) all-reduce(f32[256]{0:T(256)S(1)} %get-tuple-element.250, f32[256]{0:T(256)S(1)} %get-tuple-element.252), channel_id=1, replica_groups=mesh['tx'=4,'ty'=32] {'ty'}, use_global_device_ids=true, to_apply=%region_25.26 | all-reduce | flops 512 | bytes 4096 | tf_op jit(solution)/shard_map/psum | solution.py:268
  393.0 6.8 %all-reduce.6 = (f32[256]{0:T(256)S(1)}, f32[256]{0:T(256)S(1)}) all-reduce(f32[256]{0:T(256)S(1)} %get-tuple-element.399, f32[256]{0:T(256)S(1)} %get-tuple-element.400), channel_id=1, replica_groups=mesh['tx'=4,'ty'=32] {'tx'}, use_global_device_ids=true, to_apply=%region_26.27 | all-reduce | flops 512 | bytes 4096 | tf_op jit(solution)/shard_map/psum | solution.py:267
  401.8 31.2 %all-reduce.11.cloned.1.call-done = (f32[256,256]{1,0:T(8,128)}, f32[3,8,32,32]{3,2,1,0:T(8,128)}, f32[256,1024]{1,0:T(8,128)}, f32[1024,256]{1,0:T(8,128)}) async-done(((f32[256,256]{1,0:T(8,128)}, f32[3,8,32,32]{3,2,1,0:T(8,128)}, f32[256,1024]{1,0:T(8,128)}, f32[1024,256]{1,0:T(8,128)}), (f32[256,256]{1,0:T(8,128)}, f32[3,8,32,32]{3,2,1,0:T(8,128)}, f32[256,1024]{1,0:T(8,128)}, ...) | async-done | bytes 2457616 | tf_op jit(solution)/shard_map/psum | solution.py:268
  433.1 117.5 %while.50 = (s32[]{:T(128)}, f32[1280,256]{1,0:T(8,128)S(1)}, s32[16,1024]{1,0:T(8,128)}, f32[1024,256]{1,0:T(8,128)S(1)}, s32[]{:T(128)}) while((s32[]{:T(128)}, f32[1280,256]{1,0:T(8,128)S(1)}, s32[16,1024]{1,0:T(8,128)}, f32[1024,256]{1,0:T(8,128)S(1)}, s32[]{:T(128)}) %tuple.124), condition=%wide.region_18.19_spmd, body=%wide.region_16.18_spmd.sunk | while | flops 265218 | bytes 3158089 | solution.py:65
  433.9 6.5 %scatter_fusion = f32[1280,256]{1,0:T(8,128)S(1)} fusion(f32[1280,256]{1,0:T(8,128)S(1)} %get-tuple-element.685, s32[1024]{0:T(1024)S(1)} %bitcast.200, f32[1024,256]{1,0:T(8,128)S(1)} %get-tuple-element.692), kind=kCustom, calls=%fused_computation.6.clone.1 | custom fusion | flops 262144 | bytes 3149824 | tf_op jit(solution)/shard_map/while/body/eval_jaxpr/scatter-add | solution.py:63
  441.3 6.5 %scatter_fusion = f32[1280,256]{1,0:T(8,128)S(1)} fusion(f32[1280,256]{1,0:T(8,128)S(1)} %get-tuple-element.685, s32[1024]{0:T(1024)S(1)} %bitcast.200, f32[1024,256]{1,0:T(8,128)S(1)} %get-tuple-element.692), kind=kCustom, calls=%fused_computation.6.clone.1 | custom fusion | flops 262144 | bytes 3149824 | tf_op jit(solution)/shard_map/while/body/eval_jaxpr/scatter-add | solution.py:63
  448.6 6.5 %scatter_fusion = f32[1280,256]{1,0:T(8,128)S(1)} fusion(f32[1280,256]{1,0:T(8,128)S(1)} %get-tuple-element.685, s32[1024]{0:T(1024)S(1)} %bitcast.200, f32[1024,256]{1,0:T(8,128)S(1)} %get-tuple-element.692), kind=kCustom, calls=%fused_computation.6.clone.1 | custom fusion | flops 262144 | bytes 3149824 | tf_op jit(solution)/shard_map/while/body/eval_jaxpr/scatter-add | solution.py:63
  456.0 6.5 %scatter_fusion = f32[1280,256]{1,0:T(8,128)S(1)} fusion(f32[1280,256]{1,0:T(8,128)S(1)} %get-tuple-element.685, s32[1024]{0:T(1024)S(1)} %bitcast.200, f32[1024,256]{1,0:T(8,128)S(1)} %get-tuple-element.692), kind=kCustom, calls=%fused_computation.6.clone.1 | custom fusion | flops 262144 | bytes 3149824 | tf_op jit(solution)/shard_map/while/body/eval_jaxpr/scatter-add | solution.py:63
  463.3 6.5 %scatter_fusion = f32[1280,256]{1,0:T(8,128)S(1)} fusion(f32[1280,256]{1,0:T(8,128)S(1)} %get-tuple-element.685, s32[1024]{0:T(1024)S(1)} %bitcast.200, f32[1024,256]{1,0:T(8,128)S(1)} %get-tuple-element.692), kind=kCustom, calls=%fused_computation.6.clone.1 | custom fusion | flops 262144 | bytes 3149824 | tf_op jit(solution)/shard_map/while/body/eval_jaxpr/scatter-add | solution.py:63
  470.6 6.5 %scatter_fusion = f32[1280,256]{1,0:T(8,128)S(1)} fusion(f32[1280,256]{1,0:T(8,128)S(1)} %get-tuple-element.685, s32[1024]{0:T(1024)S(1)} %bitcast.200, f32[1024,256]{1,0:T(8,128)S(1)} %get-tuple-element.692), kind=kCustom, calls=%fused_computation.6.clone.1 | custom fusion | flops 262144 | bytes 3149824 | tf_op jit(solution)/shard_map/while/body/eval_jaxpr/scatter-add | solution.py:63
  478.0 6.5 %scatter_fusion = f32[1280,256]{1,0:T(8,128)S(1)} fusion(f32[1280,256]{1,0:T(8,128)S(1)} %get-tuple-element.685, s32[1024]{0:T(1024)S(1)} %bitcast.200, f32[1024,256]{1,0:T(8,128)S(1)} %get-tuple-element.692), kind=kCustom, calls=%fused_computation.6.clone.1 | custom fusion | flops 262144 | bytes 3149824 | tf_op jit(solution)/shard_map/while/body/eval_jaxpr/scatter-add | solution.py:63
  485.3 6.5 %scatter_fusion = f32[1280,256]{1,0:T(8,128)S(1)} fusion(f32[1280,256]{1,0:T(8,128)S(1)} %get-tuple-element.685, s32[1024]{0:T(1024)S(1)} %bitcast.200, f32[1024,256]{1,0:T(8,128)S(1)} %get-tuple-element.692), kind=kCustom, calls=%fused_computation.6.clone.1 | custom fusion | flops 262144 | bytes 3149824 | tf_op jit(solution)/shard_map/while/body/eval_jaxpr/scatter-add | solution.py:63
  492.7 6.5 %scatter_fusion = f32[1280,256]{1,0:T(8,128)S(1)} fusion(f32[1280,256]{1,0:T(8,128)S(1)} %get-tuple-element.685, s32[1024]{0:T(1024)S(1)} %bitcast.200, f32[1024,256]{1,0:T(8,128)S(1)} %get-tuple-element.692), kind=kCustom, calls=%fused_computation.6.clone.1 | custom fusion | flops 262144 | bytes 3149824 | tf_op jit(solution)/shard_map/while/body/eval_jaxpr/scatter-add | solution.py:63
  500.0 6.5 %scatter_fusion = f32[1280,256]{1,0:T(8,128)S(1)} fusion(f32[1280,256]{1,0:T(8,128)S(1)} %get-tuple-element.685, s32[1024]{0:T(1024)S(1)} %bitcast.200, f32[1024,256]{1,0:T(8,128)S(1)} %get-tuple-element.692), kind=kCustom, calls=%fused_computation.6.clone.1 | custom fusion | flops 262144 | bytes 3149824 | tf_op jit(solution)/shard_map/while/body/eval_jaxpr/scatter-add | solution.py:63
  507.4 6.5 %scatter_fusion = f32[1280,256]{1,0:T(8,128)S(1)} fusion(f32[1280,256]{1,0:T(8,128)S(1)} %get-tuple-element.685, s32[1024]{0:T(1024)S(1)} %bitcast.200, f32[1024,256]{1,0:T(8,128)S(1)} %get-tuple-element.692), kind=kCustom, calls=%fused_computation.6.clone.1 | custom fusion | flops 262144 | bytes 3149824 | tf_op jit(solution)/shard_map/while/body/eval_jaxpr/scatter-add | solution.py:63
  514.7 6.5 %scatter_fusion = f32[1280,256]{1,0:T(8,128)S(1)} fusion(f32[1280,256]{1,0:T(8,128)S(1)} %get-tuple-element.685, s32[1024]{0:T(1024)S(1)} %bitcast.200, f32[1024,256]{1,0:T(8,128)S(1)} %get-tuple-element.692), kind=kCustom, calls=%fused_computation.6.clone.1 | custom fusion | flops 262144 | bytes 3149824 | tf_op jit(solution)/shard_map/while/body/eval_jaxpr/scatter-add | solution.py:63
  522.0 6.5 %scatter_fusion = f32[1280,256]{1,0:T(8,128)S(1)} fusion(f32[1280,256]{1,0:T(8,128)S(1)} %get-tuple-element.685, s32[1024]{0:T(1024)S(1)} %bitcast.200, f32[1024,256]{1,0:T(8,128)S(1)} %get-tuple-element.692), kind=kCustom, calls=%fused_computation.6.clone.1 | custom fusion | flops 262144 | bytes 3149824 | tf_op jit(solution)/shard_map/while/body/eval_jaxpr/scatter-add | solution.py:63
  529.4 6.5 %scatter_fusion = f32[1280,256]{1,0:T(8,128)S(1)} fusion(f32[1280,256]{1,0:T(8,128)S(1)} %get-tuple-element.685, s32[1024]{0:T(1024)S(1)} %bitcast.200, f32[1024,256]{1,0:T(8,128)S(1)} %get-tuple-element.692), kind=kCustom, calls=%fused_computation.6.clone.1 | custom fusion | flops 262144 | bytes 3149824 | tf_op jit(solution)/shard_map/while/body/eval_jaxpr/scatter-add | solution.py:63
  536.7 6.5 %scatter_fusion = f32[1280,256]{1,0:T(8,128)S(1)} fusion(f32[1280,256]{1,0:T(8,128)S(1)} %get-tuple-element.685, s32[1024]{0:T(1024)S(1)} %bitcast.200, f32[1024,256]{1,0:T(8,128)S(1)} %get-tuple-element.692), kind=kCustom, calls=%fused_computation.6.clone.1 | custom fusion | flops 262144 | bytes 3149824 | tf_op jit(solution)/shard_map/while/body/eval_jaxpr/scatter-add | solution.py:63
  544.1 6.5 %scatter_fusion = f32[1280,256]{1,0:T(8,128)S(1)} fusion(f32[1280,256]{1,0:T(8,128)S(1)} %get-tuple-element.685, s32[1024]{0:T(1024)S(1)} %bitcast.200, f32[1024,256]{1,0:T(8,128)S(1)} %get-tuple-element.692), kind=kCustom, calls=%fused_computation.6.clone.1 | custom fusion | flops 262144 | bytes 3149824 | tf_op jit(solution)/shard_map/while/body/eval_jaxpr/scatter-add | solution.py:63
  559.1 4.0 collective-permute-start.4
  (319 shorter events, 174.3 us)
Async XLA Ops:
  7.2 124.3 %copy-start = (bf16[256,256]{1,0:T(8,128)(2,1)S(1)}, bf16[256,256]{1,0:T(8,128)(2,1)}, u32[]{:S(2)}) copy-start(bf16[256,256]{1,0:T(8,128)(2,1)} %param.25) | copy-start | bytes 393220
  7.2 22.1 %copy-start.1 = (s32[1,1024]{1,0:T(1,128)S(1)}, s32[1,1024]{1,0:T(1,128)}, u32[]{:S(2)}) copy-start(s32[1,1024]{1,0:T(1,128)} %param.21) | copy-start | bytes 12292
  11.1 35.9 %collective-permute-start.3 = (bf16[64,256]{0,1:T(8,128)(2,1)S(1)}, bf16[64,256]{0,1:T(8,128)(2,1)S(1)}, u32[]{:S(2)}, u32[]{:S(2)}) collective-permute-start(bf16[64,256]{0,1:T(8,128)(2,1)S(1)} %get-tuple-element.429), channel_id=1, source_target_pairs={{0,1},{1,2},{2,3},{3,4},{4,5},{5,6},{6,7},{7,8},{8,9},{9,10},{10,1... | collective-permute-start | bytes 98312 | tf_op jit(solution)/shard_map/ppermute | solution.py:17
  15.7 31.3 %collective-permute-start.2 = (bf16[64,256]{0,1:T(8,128)(2,1)S(1)}, bf16[64,256]{0,1:T(8,128)(2,1)S(1)}, u32[]{:S(2)}, u32[]{:S(2)}) collective-permute-start(bf16[64,256]{0,1:T(8,128)(2,1)S(1)} %get-tuple-element.430), channel_id=1, source_target_pairs={{1,0},{2,1},{3,2},{4,3},{5,4},{6,5},{7,6},{8,7},{9,8},{10,9},{11,1... | collective-permute-start | bytes 98312 | tf_op jit(solution)/shard_map/ppermute | solution.py:17
  17.6 29.4 %collective-permute-start.1 = (bf16[64,256]{0,1:T(8,128)(2,1)S(1)}, bf16[64,256]{0,1:T(8,128)(2,1)S(1)}, u32[]{:S(2)}, u32[]{:S(2)}) collective-permute-start(bf16[64,256]{0,1:T(8,128)(2,1)S(1)} %get-tuple-element.431), channel_id=1, source_target_pairs={{0,32},{32,64},{64,96},{1,33},{33,65},{65,97},{2,34},{34,66},{66,9... | collective-permute-start | bytes 98312 | tf_op jit(solution)/shard_map/ppermute | solution.py:17
  21.2 25.8 %collective-permute-start = (bf16[64,256]{0,1:T(8,128)(2,1)S(1)}, bf16[64,256]{0,1:T(8,128)(2,1)S(1)}, u32[]{:S(2)}, u32[]{:S(2)}) collective-permute-start(bf16[64,256]{0,1:T(8,128)(2,1)S(1)} %get-tuple-element.432), channel_id=1, source_target_pairs={{32,0},{64,32},{96,64},{33,1},{65,33},{97,65},{34,2},{66,34},{98,6... | collective-permute-start | bytes 98312 | tf_op jit(solution)/shard_map/ppermute | solution.py:17
  29.3 16.5 %copy-start.12 = (bf16[1,1024,256]{2,1,0:T(8,128)(2,1)S(1)}, bf16[1,1024,256]{2,1,0:T(8,128)(2,1)}, u32[]{:S(2)}) copy-start(bf16[1,1024,256]{2,1,0:T(8,128)(2,1)} %param.19) | copy-start | bytes 1572868
  29.3 16.7 %copy-start.15 = (bf16[1,1024,256]{2,1,0:T(8,128)(2,1)S(1)}, bf16[1,1024,256]{2,1,0:T(8,128)(2,1)}, u32[]{:S(2)}) copy-start(bf16[1,1024,256]{2,1,0:T(8,128)(2,1)} %param.31) | copy-start | bytes 1572868
  45.7 87.9 %copy-start.25 = (s32[1024]{0:T(1024)}, s32[1024]{0:T(1024)S(1)}, u32[]{:S(2)}) copy-start(s32[1024]{0:T(1024)S(1)} %get-tuple-element.414) | copy-start | bytes 12292
  49.6 83.5 %copy-start.14 = (bf16[1,1024,256]{1,2,0:T(8,128)(2,1)S(1)}, bf16[1,1024,256]{1,2,0:T(8,128)(2,1)}, u32[]{:S(2)}) copy-start(bf16[1,1024,256]{1,2,0:T(8,128)(2,1)} %copy.64) | copy-start | bytes 1572868
  131.5 8.9 %copy-start.6 = (f32[1024,256]{1,0:T(8,128)}, f32[1024,256]{1,0:T(8,128)S(1)}, u32[]{:S(2)}) copy-start(f32[1024,256]{1,0:T(8,128)S(1)} %get-tuple-element.246) | copy-start | bytes 3145732
  133.1 29.9 %copy-start.22 = (s32[1,2048]{1,0:T(1,128)S(1)}, s32[1,2048]{1,0:T(1,128)}, u32[]{:S(2)}) copy-start(s32[1,2048]{1,0:T(1,128)} %param.22) | copy-start | bytes 24580
  140.4 52.4 %all-to-all-start = ((bf16[128,16,512]{2,1,0:T(8,128)(2,1)}), bf16[128,16,512]{2,1,0:T(8,128)(2,1)S(1)}, u32[]{:S(2)}, u32[]{:S(2)}) async-start(bf16[128,16,512]{2,1,0:T(8,128)(2,1)} %bitcast.194), calls=%async_computation | async-start | bytes 4194304 | tf_op jit(solution)/shard_map/all_to_all | solution.py:228
  169.0 33.0 %copy-start.23 = (s32[2048,1]{0,1:T(1,128)}, s32[2048,1]{0,1:T(1,128)S(1)}, u32[]{:S(2)}) copy-start(s32[2048,1]{0,1:T(1,128)S(1)} %compare_select_fusion.3) | copy-start | bytes 24580
  202.0 4.6 copy-start.16
  202.0 4.6 copy-start.17
  213.4 4.7 copy-start.28
  216.1 1.9 copy-start.2
  221.9 4.9 copy-start.3
  221.9 4.9 copy-start.29
  229.8 2.1 copy-start.8
  231.9 1.3 copy-start.4
  231.9 1.9 copy-start.5
  232.9 3.0 copy-start.9
  232.9 1.3 copy-start.10
  234.3 4.3 copy-start.11
  247.4 4.7 copy-start.28
  250.1 1.9 copy-start.2
  255.9 5.2 copy-start.3
  255.9 5.2 copy-start.29
  264.1 2.1 copy-start.8
  266.2 1.3 copy-start.4
  266.2 1.9 copy-start.5
  267.2 3.0 copy-start.9
  267.2 1.3 copy-start.10
  268.6 4.3 copy-start.11
  274.9 15.9 %copy-start.26 = (s32[1024]{0:T(1024)S(1)}, s32[1024]{0:T(1024)}, u32[]{:S(2)}) copy-start(s32[1024]{0:T(1024)} %copy-done.25) | copy-start | bytes 12292
  286.4 35.0 %all-to-all-start.1 = ((bf16[128,16,512]{2,1,0:T(8,128)(2,1)}), bf16[128,16,512]{2,1,0:T(8,128)(2,1)S(1)}, u32[]{:S(2)}, u32[]{:S(2)}) async-start(bf16[128,16,512]{2,1,0:T(8,128)(2,1)} %bitcast.193), calls=%async_computation.1 | async-start | bytes 4194304 | tf_op jit(solution)/shard_map/all_to_all | solution.py:252
  290.8 142.3 %all-reduce.11.cloned.1.call-start = ((), (), s32[]{:S(2)}) async-start(), calls=%async_computation.2 | async-start | bytes 5505024 | tf_op jit(solution)/shard_map/psum | solution.py:268
  321.4 4.5 copy-start.27
  325.4 2.6 copy-start.7
  326.0 3.2 copy-start.24
  328.0 71.8 %copy-start.13 = (bf16[1024,256]{0,1:T(8,128)(2,1)}, bf16[1024,256]{0,1:T(8,128)(2,1)S(1)}, u32[]{:S(2)}) copy-start(bf16[1024,256]{0,1:T(8,128)(2,1)S(1)} %fusion.57) | copy-start | bytes 1572868
  329.1 243.3 %all-reduce.13.cloned.1.call-start = ((), (), s32[]{:S(2)}) async-start(), calls=%async_computation.3 | async-start | bytes 5505024 | tf_op jit(solution)/shard_map/psum | solution.py:267
  552.2 18.0 %collective-permute-start.7 = (bf16[64,256]{1,0:T(8,128)(2,1)S(1)}, bf16[64,256]{1,0:T(8,128)(2,1)S(1)}, u32[]{:S(2)}, u32[]{:S(2)}) collective-permute-start(bf16[64,256]{1,0:T(8,128)(2,1)S(1)} %get-tuple-element.425), channel_id=1, source_target_pairs={{1,0},{2,1},{3,2},{4,3},{5,4},{6,5},{7,6},{8,7},{9,8},{10,9},{11,1... | collective-permute-start | bytes 98312 | tf_op jit(solution)/shard_map/ppermute | solution.py:17
  555.0 13.8 %collective-permute-start.6 = (bf16[64,256]{1,0:T(8,128)(2,1)S(1)}, bf16[64,256]{1,0:T(8,128)(2,1)S(1)}, u32[]{:S(2)}, u32[]{:S(2)}) collective-permute-start(bf16[64,256]{1,0:T(8,128)(2,1)S(1)} %get-tuple-element.426), channel_id=1, source_target_pairs={{0,1},{1,2},{2,3},{3,4},{4,5},{5,6},{6,7},{7,8},{8,9},{9,10},{10,1... | collective-permute-start | bytes 98312 | tf_op jit(solution)/shard_map/ppermute | solution.py:17
  557.8 9.5 %collective-permute-start.5 = (bf16[64,256]{1,0:T(8,128)(2,1)S(1)}, bf16[64,256]{1,0:T(8,128)(2,1)S(1)}, u32[]{:S(2)}, u32[]{:S(2)}) collective-permute-start(bf16[64,256]{1,0:T(8,128)(2,1)S(1)} %get-tuple-element.427), channel_id=1, source_target_pairs={{32,0},{64,32},{96,64},{33,1},{65,33},{97,65},{34,2},{66,34},{98,6... | collective-permute-start | bytes 98312 | tf_op jit(solution)/shard_map/ppermute | solution.py:17
  559.1 6.7 %collective-permute-start.4 = (bf16[64,256]{1,0:T(8,128)(2,1)S(1)}, bf16[64,256]{1,0:T(8,128)(2,1)S(1)}, u32[]{:S(2)}, u32[]{:S(2)}) collective-permute-start(bf16[64,256]{1,0:T(8,128)(2,1)S(1)} %get-tuple-element.428), channel_id=1, source_target_pairs={{0,32},{32,64},{64,96},{1,33},{33,65},{65,97},{2,34},{34,66},{66,9... | collective-permute-start | bytes 98312 | tf_op jit(solution)/shard_map/ppermute | solution.py:17
  (4 other events, 2.5 us)
Sparse Core Ops, SparseCore 0:
  329.2 103.7 all-reduce.10
  435.8 70.0 all-reduce.12
